TPU v7x, 512 devices: a whole 4x4x16 slice. The times are simulated.
512 devices in a mesh: dp: 32 (over y, x, core), seq: 16 (over z).
Axes of the slice: x: 4, y: 4, z: 16, core: 2. Of those that a mesh axis runs over, the one named last changes fastest.
Arguments:
- tokens: bfloat16 [64, 4096, 768], P('dp', 'seq'), may hold values from -6 to 6
- norm_gain: float32 [768], replicated, may hold values from 0.1 to 1.9
- dilated_weight: bfloat16 [3, 768, 384], P(None, None, 'seq'), may hold values from -0.125 to 0.125
- output_weight: bfloat16 [384, 768], P(None, 'seq'), may hold values from -0.3125 to 0.3125
- cotangent: bfloat16 [64, 4096, 768], P('dp', 'seq'), may hold values from -6 to 6
Outputs:
- block_output: bfloat16 [64, 4096, 768], P('dp', 'seq')
- token_input_gradient: bfloat16 [64, 4096, 768], P('dp', 'seq')
- dilated_gradient: float32 [3, 768, 384], P(None, None, 'seq')
- output_gradient: float32 [384, 768], P(None, 'seq')
- gain_gradient: float32 [768], P('seq')
All inputs are finite; a program needn't handle non-finite values.
Results may differ from a plain program's by a relative error of at most 0.017.
Values may be sent and summed in bfloat16 or wider, within the bound.
No kernel may reach another device: no remote copies, remote signals or barrier semaphores. Data moves between devices by JAX's collectives and lax.ppermute only.
A program may use at most 64 MiB of HBM per device.

v0:
```python
import jax
import jax.numpy as jnp
from jax import lax
from jax.sharding import PartitionSpec as P

DILATION_STEP = 64
gelu_scale = 0.7978845608
cubic_term = 0.044715
epsilon = 1e-06


def extended(value, sides, width):
    for axis, dim in sides:
        size, length = (lax.axis_size(axis), value.shape[dim])
        up = [(i, (i + 1) % size) for i in range(size - 1)]
        down = [(j, i) for i, j in up]
        last = lax.slice_in_dim(value, length - width, length, axis=dim)
        first = lax.slice_in_dim(value, 0, width, axis=dim)
        before = lax.ppermute(last, axis, up)
        after = lax.ppermute(first, axis, down)
        value = jnp.concatenate([before, value, after], axis=dim)
    return value


def activate(value):
    inner = jnp.tanh(gelu_scale * (value + cubic_term * value * value * value))
    return 0.5 * value * (1.0 + inner)


def derivative(value):
    inner = jnp.tanh(gelu_scale * (value + cubic_term * value * value * value))
    return 0.5 * (1.0 + inner) + 0.5 * value * (1.0 - inner * inner) * gelu_scale * (
        1.0 + 3.0 * cubic_term * value * value
    )


def combine_block_parts(received, sequence_number):
    return jnp.sum(
        received.reshape(sequence_number, received.shape[0] // sequence_number, received.shape[1]),
        axis=0,
    )


def on_device(tokens, norm_gain, dilated_weight, output_weight, cotangent):
    seqs_here, local_bins, channel_count = tokens.shape
    sequence_number = lax.axis_size("seq")
    collected_dilated, collected_output = (
        lax.all_gather(
            dilated_weight.reshape(3 * channel_count, dilated_weight.shape[2]),
            "seq",
            axis=1,
            tiled=True,
        ),
        lax.all_gather(output_weight, "seq", axis=1, tiled=True),
    )
    hidden_width = collected_dilated.shape[1]
    kernel_taps = collected_dilated.reshape(3, channel_count, hidden_width)
    as_float = tokens.astype(jnp.float32)
    inverse_rms = lax.rsqrt(jnp.mean(as_float * as_float, axis=-1, keepdims=True) + epsilon)
    normed = as_float * inverse_rms * norm_gain
    gelu_activated = activate(normed).astype(jnp.bfloat16)
    padded_input = extended(gelu_activated, (("seq", 1),), DILATION_STEP)
    dilated_sum = jnp.zeros((seqs_here * local_bins, hidden_width), jnp.float32)
    for tap_index in range(3):
        dilated_sum = dilated_sum + jnp.dot(
            padded_input[
                :, tap_index * DILATION_STEP : tap_index * DILATION_STEP + local_bins
            ].reshape(-1, channel_count),
            kernel_taps[tap_index],
            preferred_element_type=jnp.float32,
        )
    dilated_sum = dilated_sum.reshape(seqs_here, local_bins, hidden_width)
    hidden = activate(dilated_sum).astype(jnp.bfloat16)
    hidden_rows = hidden.reshape(-1, hidden_width)
    projected = jnp.dot(hidden_rows, collected_output, preferred_element_type=jnp.float32)
    residual_output = (as_float + projected.reshape(seqs_here, local_bins, channel_count)).astype(
        jnp.bfloat16
    )
    cot_rows = cotangent.reshape(-1, channel_count)
    hidden_cot = jnp.einsum(
        "nc,hc->nh", cot_rows, collected_output, preferred_element_type=jnp.float32
    ).astype(jnp.bfloat16)
    output_piece = jnp.einsum(
        "nh,nc->hc", hidden_rows, cot_rows, preferred_element_type=jnp.float32
    )
    cotangent_sum = (
        hidden_cot.reshape(seqs_here, local_bins, hidden_width).astype(jnp.float32)
        * derivative(dilated_sum)
    ).astype(jnp.bfloat16)
    padded_cotangent = extended(cotangent_sum, (("seq", 1),), DILATION_STEP)
    act_cot = jnp.zeros((seqs_here * local_bins, channel_count), jnp.float32)
    dilated_pieces = []
    for tap_index in range(3):
        start_offset = (2 - tap_index) * DILATION_STEP
        piece = padded_cotangent[:, start_offset : start_offset + local_bins].reshape(
            -1, hidden_width
        )
        act_cot = act_cot + jnp.einsum(
            "nh,ch->nc", piece, kernel_taps[tap_index], preferred_element_type=jnp.float32
        )
        dilated_pieces.append(
            jnp.einsum(
                "blc,blh->ch",
                padded_input[:, tap_index * DILATION_STEP : tap_index * DILATION_STEP + local_bins],
                cotangent_sum,
                preferred_element_type=jnp.float32,
            )
        )
    act_cot = act_cot.astype(jnp.bfloat16).reshape(seqs_here, local_bins, channel_count)
    normed_cot = act_cot.astype(jnp.float32) * derivative(normed)
    scaled_cot = norm_gain * normed_cot
    token_cotangent = (
        cotangent.astype(jnp.float32)
        + inverse_rms * scaled_cot
        - as_float * inverse_rms**3 * jnp.mean(scaled_cot * as_float, axis=-1, keepdims=True)
    )
    token_cotangent = token_cotangent.astype(jnp.bfloat16)
    gain_piece = jnp.sum(normed_cot * as_float * inverse_rms, axis=(0, 1))
    dilated_piece = jnp.stack(dilated_pieces).reshape(3 * channel_count, hidden_width)
    incoming_dilated, incoming_output, incoming_gain = (
        lax.all_to_all(dilated_piece, "seq", split_axis=1, concat_axis=0, tiled=True),
        lax.all_to_all(output_piece, "seq", split_axis=1, concat_axis=0, tiled=True),
        lax.all_to_all(
            gain_piece.reshape(1, channel_count), "seq", split_axis=1, concat_axis=0, tiled=True
        ),
    )
    dilated_weight_portion = combine_block_parts(incoming_dilated, sequence_number)
    output_weight_portion = combine_block_parts(incoming_output, sequence_number)
    gain_share = combine_block_parts(incoming_gain, sequence_number)
    dilated_total, output_total, gain_total = lax.psum(
        (dilated_weight_portion, output_weight_portion, gain_share), "dp"
    )
    scale_factor = 1.0 / (seqs_here * lax.axis_size("dp"))
    return (
        residual_output,
        token_cotangent,
        (dilated_total * scale_factor).reshape(3, channel_count, -1),
        output_total * scale_factor,
        (gain_total * scale_factor).reshape(-1),
    )


def solution(mesh):
    in_specs = (
        P("dp", "seq", None),
        P(),
        P(None, None, "seq"),
        P(None, "seq"),
        P("dp", "seq", None),
    )
    out_specs = (
        P("dp", "seq", None),
        P("dp", "seq", None),
        P(None, None, "seq"),
        P(None, "seq"),
        P("seq"),
    )
    return jax.shard_map(
        on_device, mesh=mesh, in_specs=in_specs, out_specs=out_specs, check_vma=False
    )
```

profile of v0, /device:TPU:1, one launch (start us, length us, event | category | flops | bytes accessed | tf_op | source)
XLA Modules:
  0.0 478.6 jit_solution(10501041938618014832)
XLA Ops:
  7.2 1.6 copy.32
  8.9 1.4 fusion.6
  10.9 1.4 fusion.11
  12.3 4.4 collective-permute-start
  16.7 1.3 collective-permute-start.1
  19.2 35.4 %all_gather.7 = bf16[384,768]{0,1:T(8,128)(2,1)S(1)} all-gather(bf16[384,48]{0,1:T(8,128)(2,1)S(1)} %copy-done.11), channel_id=1, replica_groups=mesh['dp'=32,'seq'=16] {'seq'}, dimensions={1}, use_global_device_ids=true | all-gather | bytes 626688 | tf_op jit(solution)/shard_map/all_gather | solution.py:54
  54.6 1.5 fusion.21
  57.1 22.8 %all-gather.2.cloned.1.call-done = bf16[2304,384]{0,1:T(8,128)(2,1)} async-done(((bf16[2304,24]{0,1:T(8,128)(2,1)}), bf16[2304,384]{0,1:T(8,128)(2,1)}) %all-gather.2.cloned.1.call-update) | async-done | bytes 1769488 | tf_op jit(solution)/shard_map/all_gather | solution.py:48
  79.9 1.8 fusion.39
  82.8 1.5 multiply_convert_fusion
  84.9 3.3 collective-permute-start.3
  88.2 1.3 collective-permute-start.2
  90.5 3.1 collective-permute-done.2
  94.9 2.4 fusion.19
  98.0 7.4 %all-to-all-start.2 = ((f32[1,16,48]{2,0,1:T(1,128)}), f32[1,16,48]{2,0,1:T(1,128)S(1)}, u32[]{:S(2)}, u32[]{:S(2)}) async-start(f32[1,16,48]{2,0,1:T(1,128)} %all_to_all.31), calls=%async_computation.2 | async-start | bytes 16384 | tf_op jit(solution)/shard_map/all_to_all | solution.py:123
  105.4 2.9 fusion.51
  108.3 8.4 %all-to-all-done.2 = f32[1,16,48]{2,0,1:T(1,128)S(1)} async-done(((f32[1,16,48]{2,0,1:T(1,128)}), f32[1,16,48]{2,0,1:T(1,128)S(1)}, u32[]{:S(2)}, u32[]{:S(2)}) %all-to-all-start.2) | async-done | bytes 3104 | tf_op jit(solution)/shard_map/all_to_all | solution.py:123
  116.6 4.4 all-to-all-start.1
  121.0 1.7 convolution_bitcast_fusion
  124.5 2.0 pad_maximum_fusion
  126.5 6.4 %copy.25 = f32[3,768,384]{1,0,2:T(4,128)} copy(f32[3,768,384]{2,1,0:T(8,128)} %pad_maximum_fusion) | data formatting | bytes 7077888 | tf_op jit(solution)/shard_map/stack | solution.py:119
  133.0 6.6 %all_to_all.13 = f32[2304,16,24]{0,2,1:T(8,128)} reshape(f32[3,768,384]{1,0,2:T(4,128)} %copy.25) | data formatting | bytes 7077888 | tf_op jit(solution)/shard_map/all_to_all | solution.py:121
  139.6 22.8 %all-to-all-done.1 = f32[384,16,48]{0,2,1:T(8,128)} async-done(((f32[384,16,48]{0,2,1:T(8,128)}), f32[384,16,48]{0,2,1:T(8,128)}, u32[]{:S(2)}, u32[]{:S(2)}) %all-to-all-start.1) | async-done | bytes 1179680 | tf_op jit(solution)/shard_map/all_to_all | solution.py:122
  162.4 17.7 %all-to-all-start = ((f32[2304,16,24]{0,2,1:T(8,128)}), f32[2304,16,24]{0,2,1:T(8,128)}, u32[]{:S(2)}, u32[]{:S(2)}) async-start(f32[2304,16,24]{0,2,1:T(8,128)} %all_to_all.13), calls=%async_computation | async-start | bytes 7077888 | tf_op jit(solution)/shard_map/all_to_all | solution.py:121
  180.2 1.5 fusion.13
  181.6 2.5 fusion.16
  184.2 70.6 %psum.23 = f32[1,48]{1,0:T(1,128)S(1)} all-reduce(f32[1,48]{1,0:T(1,128)S(1)} %bitcast.73), channel_id=1, replica_groups=mesh['dp'=32,'seq'=16] {'dp'}, use_global_device_ids=true, to_apply=%region_8.0 | all-reduce | flops 48 | bytes 384 | tf_op jit(solution)/shard_map/psum | solution.py:130
  254.7 2.0 reduce_sum.59
  256.7 77.1 %all-to-all-done = f32[2304,16,24]{0,2,1:T(8,128)} async-done(((f32[2304,16,24]{0,2,1:T(8,128)}), f32[2304,16,24]{0,2,1:T(8,128)}, u32[]{:S(2)}, u32[]{:S(2)}) %all-to-all-start) | async-done | bytes 3538976 | tf_op jit(solution)/shard_map/all_to_all | solution.py:121
  333.8 2.9 reduce_sum.58
  337.2 131.4 %all-reduce.3.cloned.1.call-done = (f32[2304,24]{0,1:T(8,128)}, f32[384,48]{0,1:T(8,128)}) async-done(((f32[2304,24]{0,1:T(8,128)}, f32[384,48]{0,1:T(8,128)}), (f32[2304,24]{0,1:T(8,128)}, f32[384,48]{0,1:T(8,128)})) %all-reduce.3.cloned.1.call-update) | async-done | bytes 294928 | tf_op jit(solution)/shard_map/psum | solution.py:130
  470.2 1.5 broadcast_multiply_fusion.1
  (54 shorter events, 11.5 us)
Async XLA Ops:
  7.2 3.7 copy-start
  7.2 72.7 %all-gather.2.cloned.1.call-start = ((), (), s32[]{:S(2)}) async-start(), calls=%async_computation.3 | async-start | bytes 1880064 | tf_op jit(solution)/shard_map/all_gather | solution.py:48
  8.9 9.1 %copy-start.1 = (bf16[2,256,768]{2,1,0:T(8,128)(2,1)S(1)}, bf16[2,256,768]{2,1,0:T(8,128)(2,1)}, u32[]{:S(2)}) copy-start(bf16[2,256,768]{2,1,0:T(8,128)(2,1)} %param.9) | copy-start | bytes 2359300
  12.3 6.9 %copy-start.11 = (bf16[384,48]{0,1:T(8,128)(2,1)S(1)}, bf16[384,48]{0,1:T(8,128)(2,1)}, u32[]{:S(2)}) copy-start(bf16[384,48]{0,1:T(8,128)(2,1)} %param.8) | copy-start | bytes 110596
  12.3 43.8 %collective-permute-start = (bf16[2,64,768]{2,1,0:T(8,128)(2,1)S(1)}, bf16[2,64,768]{2,1,0:T(8,128)(2,1)S(1)}, u32[]{:S(2)}, u32[]{:S(2)}) collective-permute-start(bf16[2,64,768]{2,1,0:T(8,128)(2,1)S(1)} %get-tuple-element.21), channel_id=1, source_target_pairs={{0,1},{1,2},{2,3},{3,4},{4,5},{5,6},{6,7},{7,8},{8,9},{9,10},{10,1... | collective-permute-start | bytes 589832 | tf_op jit(solution)/shard_map/ppermute | solution.py:19
  16.7 39.4 %collective-permute-start.1 = (bf16[2,64,768]{2,1,0:T(8,128)(2,1)S(1)}, bf16[2,64,768]{2,1,0:T(8,128)(2,1)S(1)}, u32[]{:S(2)}, u32[]{:S(2)}) collective-permute-start(bf16[2,64,768]{2,1,0:T(8,128)(2,1)S(1)} %get-tuple-element.22), channel_id=1, source_target_pairs={{1,0},{2,1},{3,2},{4,3},{5,4},{6,5},{7,6},{8,7},{9,8},{10,9},{11,1... | collective-permute-start | bytes 589832 | tf_op jit(solution)/shard_map/ppermute | solution.py:20
  54.6 1.5 copy-start.3
  57.1 25.2 %copy-start.2 = (bf16[2,256,768]{2,1,0:T(8,128)(2,1)}, bf16[2,256,768]{2,1,0:T(8,128)(2,1)S(1)}, u32[]{:S(2)}) copy-start(bf16[2,256,768]{2,1,0:T(8,128)(2,1)S(1)} %get-tuple-element.20) | copy-start | bytes 2359300
  79.9 1.8 copy-start.5
  81.7 1.1 copy-start.7
  82.8 1.5 copy-start.6
  84.9 5.6 %collective-permute-start.3 = (bf16[2,64,384]{2,1,0:T(8,128)(2,1)S(1)}, bf16[2,64,384]{2,1,0:T(8,128)(2,1)S(1)}, u32[]{:S(2)}, u32[]{:S(2)}) collective-permute-start(bf16[2,64,384]{2,1,0:T(8,128)(2,1)S(1)} %get-tuple-element.25), channel_id=1, source_target_pairs={{0,1},{1,2},{2,3},{3,4},{4,5},{5,6},{6,7},{7,8},{8,9},{9,10},{10,1... | collective-permute-start | bytes 294920 | tf_op jit(solution)/shard_map/ppermute | solution.py:19
  88.2 5.4 %collective-permute-start.2 = (bf16[2,64,384]{2,1,0:T(8,128)(2,1)S(1)}, bf16[2,64,384]{2,1,0:T(8,128)(2,1)S(1)}, u32[]{:S(2)}, u32[]{:S(2)}) collective-permute-start(bf16[2,64,384]{2,1,0:T(8,128)(2,1)S(1)} %get-tuple-element.26), channel_id=1, source_target_pairs={{1,0},{2,1},{3,2},{4,3},{5,4},{6,5},{7,6},{8,7},{9,8},{10,9},{11,1... | collective-permute-start | bytes 294920 | tf_op jit(solution)/shard_map/ppermute | solution.py:20
  94.2 0.7 copy-start.10
  98.0 18.7 %all-to-all-start.2 = ((f32[1,16,48]{2,0,1:T(1,128)}), f32[1,16,48]{2,0,1:T(1,128)S(1)}, u32[]{:S(2)}, u32[]{:S(2)}) async-start(f32[1,16,48]{2,0,1:T(1,128)} %all_to_all.31), calls=%async_computation.2 | async-start | bytes 16384 | tf_op jit(solution)/shard_map/all_to_all | solution.py:123
  116.6 45.7 %all-to-all-start.1 = ((f32[384,16,48]{0,2,1:T(8,128)}), f32[384,16,48]{0,2,1:T(8,128)}, u32[]{:S(2)}, u32[]{:S(2)}) async-start(f32[384,16,48]{0,2,1:T(8,128)} %fusion.51), calls=%async_computation.1 | async-start | bytes 2359296 | tf_op jit(solution)/shard_map/all_to_all | solution.py:122
  122.8 1.1 copy-start.8
  139.6 40.5 %copy-start.4 = (bf16[384,768]{0,1:T(8,128)(2,1)S(1)}, bf16[384,768]{0,1:T(8,128)(2,1)}, u32[]{:S(2)}) copy-start(bf16[384,768]{0,1:T(8,128)(2,1)} %copy-done.3) | copy-start | bytes 1769476
  139.6 40.5 %copy-start.9 = (bf16[512,384]{1,0:T(8,128)(2,1)S(1)}, bf16[512,384]{1,0:T(8,128)(2,1)}, u32[]{:S(2)}) copy-start(bf16[512,384]{1,0:T(8,128)(2,1)} %get-tuple-element.29) | copy-start | bytes 1179652
  162.4 171.4 %all-to-all-start = ((f32[2304,16,24]{0,2,1:T(8,128)}), f32[2304,16,24]{0,2,1:T(8,128)}, u32[]{:S(2)}, u32[]{:S(2)}) async-start(f32[2304,16,24]{0,2,1:T(8,128)} %all_to_all.13), calls=%async_computation | async-start | bytes 7077888 | tf_op jit(solution)/shard_map/all_to_all | solution.py:121
  180.1 1.6 copy-start.12
  180.1 1.6 copy-start.13
  180.1 288.5 %all-reduce.3.cloned.1.call-start = ((), (), s32[]{:S(2)}) async-start(), calls=%async_computation.4 | async-start | bytes 589824 | tf_op jit(solution)/shard_map/psum | solution.py:130
Sparse Core Ops, SparseCore 0:
  10.7 69.1 all-gather.1
  336.8 131.7 all-reduce.2
where the time goes:
time: 480 us; the launch traced here: 479 us
  waiting for transfers between devices  266 us (55%)
  blocking collectives  106 us (22%)
  starting transfers between devices  39.9 us (8%)
  other arithmetic  19.7 us (4%)
  local copies, waits for them, and re-layouts  18.5 us (4%)
  matrix products  14.7 us (3%)
  between operations  14.3 us (3%)
    psum x1, waiting for transfers between devices, on_device(): lax.psum((dilated_weight_portion, output_weight_portion, gain_share), 'dp')  131 us
    all_to_all x1, waiting for transfers between devices, on_device(): lax.all_to_all(dilated_piece, 'seq', split_axis=1, concat_axis=0, tiled=T...  77.1 us
    psum x1, blocking collectives, on_device(): lax.psum((dilated_weight_portion, output_weight_portion, gain_share), 'dp')  70.6 us
    all_gather x1, blocking collectives, on_device(): lax.all_gather(output_weight, 'seq', axis=1, tiled=True)  35.4 us
    all_gather x1, waiting for transfers between devices, on_device(): lax.all_gather(dilated_weight.reshape(3 * channel_count, dilated_weight.s...  22.8 us
    all_to_all x1, waiting for transfers between devices, on_device(): lax.all_to_all(output_piece, 'seq', split_axis=1, concat_axis=0, tiled=True)  22.8 us
    all_to_all x1, starting transfers between devices, on_device(): lax.all_to_all(dilated_piece, 'seq', split_axis=1, concat_axis=0, tiled=T...  17.7 us
  transfers between devices with their start and end apart: 9, of which 6 were waited for; matrix products, arithmetic and copies ran while one was open for 6% of the time, Pallas kernels for 0%

commit v1 on v0

--- a/solution.py
+++ b/solution.py
@@ -45,11 +45,17 @@
     seqs_here, local_bins, channel_count = tokens.shape
     sequence_number = lax.axis_size("seq")
     collected_dilated, collected_output = (
-        lax.all_gather(
-            dilated_weight.reshape(3 * channel_count, dilated_weight.shape[2]),
-            "seq",
+        jnp.concatenate(
+            lax.all_to_all(
+                jnp.stack(
+                    [dilated_weight.reshape(3 * channel_count, dilated_weight.shape[2])]
+                    * lax.axis_size("seq")
+                ),
+                "seq",
+                0,
+                0,
+            ),
             axis=1,
-            tiled=True,
         ),
         lax.all_gather(output_weight, "seq", axis=1, tiled=True),
     )

time: 480 us -> 537 us (1.12)
  blocking collectives: 106 us -> 164 us
  waiting for transfers between devices: 266 us -> 248 us
  starting transfers between devices: 39.9 us -> 54.5 us
    all_gather x1, blocking collectives: 35.4 us -> 94.3 us  [on_device(): lax.all_gather(output_weight, 'seq', axis=1, tiled=True)]
    all_gather x1 -> x0, waiting for transfers between devices: 22.8 us -> none  [on_device(): lax.all_gather(dilated_weight.reshape(3 * channel_count, dilated_weight.s...]
    all_to_all x0 -> x1, starting transfers between devices: none -> 15.9 us  [on_device(): lax.all_to_all(jnp.stack([dilated_weight.reshape(3 * channel_count, dilat...]
    all_to_all x1, waiting for transfers between devices: 22.8 us -> 29.9 us  [on_device(): lax.all_to_all(output_piece, 'seq', split_axis=1, concat_axis=0, tiled=True)]
  transfers between devices with their start and end apart: 9 -> 9, of which waited for: 6 -> 5; matrix products, arithmetic and copies ran while one was open for 6% -> 6% of each run, Pallas kernels for 0% -> 0%
where the time goes in v1:
time: 537 us; the launch traced here: 536 us
  waiting for transfers between devices  248 us (46%)
  blocking collectives  164 us (31%)
  starting transfers between devices  54.5 us (10%)
  local copies, waits for them, and re-layouts  23.2 us (4%)
  other arithmetic  19.1 us (4%)
  between operations  14.3 us (3%)
  matrix products  12.6 us (2%)
    psum x1, waiting for transfers between devices, on_device(): lax.psum((dilated_weight_portion, output_weight_portion, gain_share), 'dp')  132 us
    all_gather x1, blocking collectives, on_device(): lax.all_gather(output_weight, 'seq', axis=1, tiled=True)  94.3 us
    all_to_all x1, waiting for transfers between devices, on_device(): lax.all_to_all(dilated_piece, 'seq', split_axis=1, concat_axis=0, tiled=T...  77.8 us
    psum x1, blocking collectives, on_device(): lax.psum((dilated_weight_portion, output_weight_portion, gain_share), 'dp')  69.8 us
    all_to_all x1, waiting for transfers between devices, on_device(): lax.all_to_all(output_piece, 'seq', split_axis=1, concat_axis=0, tiled=True)  29.9 us
    all_to_all x1, starting transfers between devices, on_device(): lax.all_to_all(jnp.stack([dilated_weight.reshape(3 * channel_count, dilat...  15.9 us
    all_to_all x1, starting transfers between devices, on_device(): lax.all_to_all(dilated_piece, 'seq', split_axis=1, concat_axis=0, tiled=T...  12.4 us
    all_to_all x1, starting transfers between devices, on_device(): lax.all_to_all(gain_piece.reshape(1, channel_count), 'seq', split_axis=1,...  11.3 us
  transfers between devices with their start and end apart: 9, of which 5 were waited for; matrix products, arithmetic and copies ran while one was open for 6% of the time, Pallas kernels for 0%

profile of v1, /device:TPU:1, one launch (start us, length us, event | category | flops | bytes accessed | tf_op | source)
XLA Modules:
  0.0 536.1 jit_solution(8939125817442943455)
XLA Ops:
  7.2 0.9 copy.32
  8.1 1.4 stack.15
  9.4 15.9 %all-to-all-start = ((bf16[16,2304,24]{1,2,0:T(8,128)(2,1)}), bf16[16,2304,24]{1,2,0:T(8,128)(2,1)S(1)}, u32[]{:S(2)}, u32[]{:S(2)}) async-start(bf16[16,2304,24]{1,2,0:T(8,128)(2,1)} %stack.15), calls=%async_computation | async-start | bytes 3538944 | tf_op jit(solution)/shard_map/all_to_all | solution.py:49
  27.5 3.9 collective-permute-start
  31.5 1.3 collective-permute-start.1
  32.7 2.3 copy.26
  35.1 94.3 %all_gather.3 = bf16[384,768]{0,1:T(8,128)(2,1)S(1)} all-gather(bf16[384,48]{0,1:T(8,128)(2,1)} %param.8), channel_id=1, replica_groups=mesh['dp'=32,'seq'=16] {'seq'}, dimensions={1}, use_global_device_ids=true | all-gather | bytes 626688 | tf_op jit(solution)/shard_map/all_gather | solution.py:60
  130.1 2.6 fusion.21
  132.8 2.3 pad_maximum_fusion.2
  135.1 1.0 copy-done.2
  139.6 1.3 collective-permute-start.2
  140.9 4.0 collective-permute-start.3
  144.9 0.9 fusion.39
  147.7 2.4 fusion.19
  150.8 11.3 %all-to-all-start.3 = ((f32[1,16,48]{2,0,1:T(1,128)}), f32[1,16,48]{2,0,1:T(1,128)S(1)}, u32[]{:S(2)}, u32[]{:S(2)}) async-start(f32[1,16,48]{2,0,1:T(1,128)} %all_to_all.35), calls=%async_computation.3 | async-start | bytes 16384 | tf_op jit(solution)/shard_map/all_to_all | solution.py:129
  162.1 2.7 fusion.37
  164.9 8.5 %all-to-all-done.3 = f32[1,16,48]{2,0,1:T(1,128)S(1)} async-done(((f32[1,16,48]{2,0,1:T(1,128)}), f32[1,16,48]{2,0,1:T(1,128)S(1)}, u32[]{:S(2)}, u32[]{:S(2)}) %all-to-all-start.3) | async-done | bytes 3104 | tf_op jit(solution)/shard_map/all_to_all | solution.py:129
  173.3 4.4 all-to-all-start.2
  180.1 2.0 pad_maximum_fusion
  182.1 6.4 %copy.25 = f32[3,768,384]{1,0,2:T(4,128)} copy(f32[3,768,384]{2,1,0:T(8,128)} %pad_maximum_fusion) | data formatting | bytes 7077888 | tf_op jit(solution)/shard_map/stack | solution.py:125
  188.6 6.6 %all_to_all.32 = f32[2304,16,24]{0,2,1:T(8,128)} reshape(f32[3,768,384]{1,0,2:T(4,128)} %copy.25) | data formatting | bytes 7077888 | tf_op jit(solution)/shard_map/all_to_all | solution.py:127
  195.2 29.9 %all-to-all-done.2 = f32[384,16,48]{0,2,1:T(8,128)} async-done(((f32[384,16,48]{0,2,1:T(8,128)}), f32[384,16,48]{0,2,1:T(8,128)}, u32[]{:S(2)}, u32[]{:S(2)}) %all-to-all-start.2) | async-done | bytes 1179680 | tf_op jit(solution)/shard_map/all_to_all | solution.py:128
  225.1 12.4 %all-to-all-start.1 = ((f32[2304,16,24]{0,2,1:T(8,128)}), f32[2304,16,24]{0,2,1:T(8,128)}, u32[]{:S(2)}, u32[]{:S(2)}) async-start(f32[2304,16,24]{0,2,1:T(8,128)} %all_to_all.32), calls=%async_computation.1 | async-start | bytes 7077888 | tf_op jit(solution)/shard_map/all_to_all | solution.py:127
  237.5 1.5 fusion.13
  239.0 2.5 fusion.16
  241.6 69.8 %psum.23 = f32[1,48]{1,0:T(1,128)S(1)} all-reduce(f32[1,48]{1,0:T(1,128)S(1)} %bitcast.90), channel_id=1, replica_groups=mesh['dp'=32,'seq'=16] {'dp'}, use_global_device_ids=true, to_apply=%region_8.0 | all-reduce | flops 48 | bytes 384 | tf_op jit(solution)/shard_map/psum | solution.py:136
  311.4 2.0 reduce_sum.59
  313.4 77.8 %all-to-all-done.1 = f32[2304,16,24]{0,2,1:T(8,128)} async-done(((f32[2304,16,24]{0,2,1:T(8,128)}), f32[2304,16,24]{0,2,1:T(8,128)}, u32[]{:S(2)}, u32[]{:S(2)}) %all-to-all-start.1) | async-done | bytes 3538976 | tf_op jit(solution)/shard_map/all_to_all | solution.py:127
  391.1 2.9 reduce_sum.58
  394.5 131.5 %all-reduce.3.cloned.1.call-done = (f32[2304,24]{0,1:T(8,128)}, f32[384,48]{0,1:T(8,128)}) async-done(((f32[2304,24]{0,1:T(8,128)}, f32[384,48]{0,1:T(8,128)}), (f32[2304,24]{0,1:T(8,128)}, f32[384,48]{0,1:T(8,128)})) %all-reduce.3.cloned.1.call-update) | async-done | bytes 294928 | tf_op jit(solution)/shard_map/psum | solution.py:136
  526.1 1.0 broadcast_multiply_fusion
  527.7 1.5 broadcast_multiply_fusion.1
  (55 shorter events, 12.7 us)
Async XLA Ops:
  9.4 15.9 %copy-start = (bf16[2,256,768]{2,1,0:T(8,128)(2,1)S(1)}, bf16[2,256,768]{2,1,0:T(8,128)(2,1)}, u32[]{:S(2)}) copy-start(bf16[2,256,768]{2,1,0:T(8,128)(2,1)} %param.5) | copy-start | bytes 2359300
  9.4 16.7 %copy-start.11 = (f32[768]{0:T(1024)S(1)}, f32[768]{0:T(1024)}, u32[]{:S(2)}) copy-start(f32[768]{0:T(1024)} %param.6) | copy-start | bytes 9220
  9.4 125.6 %all-to-all-start = ((bf16[16,2304,24]{1,2,0:T(8,128)(2,1)}), bf16[16,2304,24]{1,2,0:T(8,128)(2,1)S(1)}, u32[]{:S(2)}, u32[]{:S(2)}) async-start(bf16[16,2304,24]{1,2,0:T(8,128)(2,1)} %stack.15), calls=%async_computation | async-start | bytes 3538944 | tf_op jit(solution)/shard_map/all_to_all | solution.py:49
  27.5 105.2 %collective-permute-start = (bf16[2,64,768]{2,1,0:T(8,128)(2,1)}, bf16[2,64,768]{2,1,0:T(8,128)(2,1)}, u32[]{:S(2)}, u32[]{:S(2)}) collective-permute-start(bf16[2,64,768]{2,1,0:T(8,128)(2,1)} %get-tuple-element.24), channel_id=1, source_target_pairs={{0,1},{1,2},{2,3},{3,4},{4,5},{5,6},{6,7},{7,8},{8,9},{9,10},{10,1... | collective-permute-start | bytes 589832 | tf_op jit(solution)/shard_map/ppermute | solution.py:19
  31.5 101.3 %collective-permute-start.1 = (bf16[2,64,768]{2,1,0:T(8,128)(2,1)S(1)}, bf16[2,64,768]{2,1,0:T(8,128)(2,1)}, u32[]{:S(2)}, u32[]{:S(2)}) collective-permute-start(bf16[2,64,768]{2,1,0:T(8,128)(2,1)S(1)} %get-tuple-element.25), channel_id=1, source_target_pairs={{1,0},{2,1},{3,2},{4,3},{5,4},{6,5},{7,6},{8,7},{9,8},{10,9},{11,1... | collective-permute-start | bytes 589832 | tf_op jit(solution)/shard_map/ppermute | solution.py:20
  129.3 0.8 copy-start.6
  135.0 1.1 copy-start.2
  136.8 1.1 copy-start.4
  137.9 1.1 copy-start.8
  138.6 23.5 %copy-start.9 = (bf16[512,384]{1,0:T(8,128)(2,1)}, bf16[512,384]{1,0:T(8,128)(2,1)S(1)}, u32[]{:S(2)}) copy-start(bf16[512,384]{1,0:T(8,128)(2,1)S(1)} %get-tuple-element.32) | copy-start | bytes 1179652
  139.6 6.2 %collective-permute-start.2 = (bf16[2,64,384]{2,1,0:T(8,128)(2,1)S(1)}, bf16[2,64,384]{2,1,0:T(8,128)(2,1)S(1)}, u32[]{:S(2)}, u32[]{:S(2)}) collective-permute-start(bf16[2,64,384]{2,1,0:T(8,128)(2,1)S(1)} %get-tuple-element.28), channel_id=1, source_target_pairs={{1,0},{2,1},{3,2},{4,3},{5,4},{6,5},{7,6},{8,7},{9,8},{10,9},{11,1... | collective-permute-start | bytes 294920 | tf_op jit(solution)/shard_map/ppermute | solution.py:20
  140.9 5.6 %collective-permute-start.3 = (bf16[2,64,384]{2,1,0:T(8,128)(2,1)S(1)}, bf16[2,64,384]{2,1,0:T(8,128)(2,1)S(1)}, u32[]{:S(2)}, u32[]{:S(2)}) collective-permute-start(bf16[2,64,384]{2,1,0:T(8,128)(2,1)S(1)} %get-tuple-element.29), channel_id=1, source_target_pairs={{0,1},{1,2},{2,3},{3,4},{4,5},{5,6},{6,7},{7,8},{8,9},{9,10},{10,1... | collective-permute-start | bytes 294920 | tf_op jit(solution)/shard_map/ppermute | solution.py:19
  150.8 22.6 %all-to-all-start.3 = ((f32[1,16,48]{2,0,1:T(1,128)}), f32[1,16,48]{2,0,1:T(1,128)S(1)}, u32[]{:S(2)}, u32[]{:S(2)}) async-start(f32[1,16,48]{2,0,1:T(1,128)} %all_to_all.35), calls=%async_computation.3 | async-start | bytes 16384 | tf_op jit(solution)/shard_map/all_to_all | solution.py:129
  164.9 12.9 %copy-start.3 = (bf16[2,256,768]{2,1,0:T(8,128)(2,1)S(1)}, bf16[2,256,768]{2,1,0:T(8,128)(2,1)}, u32[]{:S(2)}) copy-start(bf16[2,256,768]{2,1,0:T(8,128)(2,1)} %get-tuple-element.23) | copy-start | bytes 2359300
  173.3 51.7 %all-to-all-start.2 = ((f32[384,16,48]{0,2,1:T(8,128)}), f32[384,16,48]{0,2,1:T(8,128)}, u32[]{:S(2)}, u32[]{:S(2)}) async-start(f32[384,16,48]{0,2,1:T(8,128)} %fusion.37), calls=%async_computation.2 | async-start | bytes 2359296 | tf_op jit(solution)/shard_map/all_to_all | solution.py:128
  178.3 1.1 copy-start.5
  195.2 42.3 %copy-start.7 = (bf16[384,768]{0,1:T(8,128)(2,1)S(1)}, bf16[384,768]{0,1:T(8,128)(2,1)}, u32[]{:S(2)}) copy-start(bf16[384,768]{0,1:T(8,128)(2,1)} %copy-done.6) | copy-start | bytes 1769476
  195.2 42.3 %copy-start.10 = (bf16[512,384]{1,0:T(8,128)(2,1)S(1)}, bf16[512,384]{1,0:T(8,128)(2,1)}, u32[]{:S(2)}) copy-start(bf16[512,384]{1,0:T(8,128)(2,1)} %copy-done.9) | copy-start | bytes 1179652
  225.1 166.1 %all-to-all-start.1 = ((f32[2304,16,24]{0,2,1:T(8,128)}), f32[2304,16,24]{0,2,1:T(8,128)}, u32[]{:S(2)}, u32[]{:S(2)}) async-start(f32[2304,16,24]{0,2,1:T(8,128)} %all_to_all.32), calls=%async_computation.1 | async-start | bytes 7077888 | tf_op jit(solution)/shard_map/all_to_all | solution.py:127
  237.4 1.6 copy-start.12
  237.4 1.6 copy-start.1
  237.5 1.6 copy-start.13
  237.5 288.6 %all-reduce.3.cloned.1.call-start = ((), (), s32[]{:S(2)}) async-start(), calls=%async_computation.4 | async-start | bytes 589824 | tf_op jit(solution)/shard_map/psum | solution.py:136
Sparse Core Ops, SparseCore 0:
  394.1 131.8 all-reduce.2
